TPU v7x, 128 devices: a whole 4x4x4 slice. The times are simulated.
128 devices in a mesh: term: 32 (over y_lo, x, z), pair: 4 (over y_hi, core).
Axes of the slice: x: 4, y: 4 (y_hi: 2, y_lo: 2; y = y_hi * 2 + y_lo), z: 4, core: 2. Of those that a mesh axis runs over, the one named last changes fastest.
Arguments:
- core_rows: bfloat16 [12288, 256], P(('term', 'pair')), may hold values from -0.25 to 0.25
- norm_ops: bfloat16 [2048, 512, 512], P(('term', 'pair')), may hold values from -6 to 6
- norm_sectors: int32 [2048, 2], P(('term', 'pair')), may hold values from 0 to 23
- comp_ops: bfloat16 [2048, 512, 512], P(('term', 'pair')), may hold values from -1.5 to 1.5
- comp_sectors: int32 [2048, 2], P(('term', 'pair')), may hold values from 0 to 23
- comp_group: int32 [2048, 1], P(('term', 'pair')), may hold values from 0 to 3; in each aligned block of 16 rows (0 to 15, 16 to 31, ...) at most 8 rows name the same one
- comp_slot: int32 [2048], P(('term', 'pair')), may hold values from 0 to 31
Outputs:
- normal_rotated: bfloat16 [2048, 256, 256], P(('term', 'pair'))
- comp_rotated: bfloat16 [4, 32, 256, 256], P('pair', 'term')
Inputs may be any that keep to these rules, and one draw needn't show every extreme that they name: `comp_group`: among the complementary tiles of one device (aligned blocks of 16 rows), at most 8 name the same owner group, a bound that some block reaches of them.
All inputs are finite; a program needn't handle non-finite values.
Results may differ from a plain program's by a relative error of at most 0.017.
Values may be sent and summed in bfloat16 or wider, within the bound.
No kernel may reach another device: no remote copies, remote signals or barrier semaphores. Data moves between devices by JAX's collectives and lax.ppermute only.
A program may use at most 128 MiB of HBM per device.

v0:
```python
import jax
import jax.numpy as jnp
from jax import lax
from jax.sharding import PartitionSpec as P

PAIR_DEV = 1


def rotate_tiles(core_tiles, op_tiles, sector_ids):
    left_rot = core_tiles[sector_ids[:, 0]]
    right_rot = core_tiles[sector_ids[:, 1]]
    half_rotated = jnp.einsum(
        "nab,nbc->nac", op_tiles, right_rot, preferred_element_type=jnp.float32
    ).astype(jnp.bfloat16)
    return jnp.einsum("nba,nbc->nac", left_rot, half_rotated, preferred_element_type=jnp.float32)


def on_device(core_rows, norm_ops, norm_sectors, comp_ops, comp_sectors, comp_group, comp_slot):
    tile_width = core_rows.shape[1]
    row_width = norm_ops.shape[1]
    gathered = lax.all_gather(core_rows, ("term", "pair"), axis=0, tiled=True)
    core_tiles = gathered.reshape(-1, row_width, tile_width)
    normal_rotated = rotate_tiles(core_tiles, norm_ops, norm_sectors).astype(jnp.bfloat16)
    groups = lax.axis_size("pair")
    term_count = lax.axis_size("term")
    comp_count = comp_ops.shape[0]
    capacity = comp_count // 2
    owned_slots = PAIR_DEV * term_count
    group_ids = comp_group[:, 0]
    member = (group_ids[:, None] == jnp.arange(groups, dtype=jnp.int32)[None, :]).astype(jnp.int32)
    before = jnp.cumsum(member, axis=0) - member
    target = group_ids * capacity + jnp.sum(before * member, axis=1)
    dispatch = target[None, :] == jnp.arange(groups * capacity, dtype=jnp.int32)[:, None]
    dispatch_bf = dispatch.astype(jnp.bfloat16)
    slots_out = (jnp.sum(jnp.where(dispatch, comp_slot[None, :] + 1, 0), axis=1) - 1).reshape(
        groups, capacity
    )
    rotated = (
        rotate_tiles(core_tiles, comp_ops, comp_sectors)
        .astype(jnp.bfloat16)
        .reshape(comp_count, -1)
    )
    outgoing = jnp.dot(dispatch_bf, rotated, preferred_element_type=jnp.float32)
    outgoing = outgoing.astype(jnp.bfloat16).reshape(groups, capacity, tile_width * tile_width)
    received, slots_in = (
        lax.all_to_all(outgoing, "pair", split_axis=0, concat_axis=0, tiled=True),
        lax.all_to_all(slots_out, "pair", split_axis=0, concat_axis=0, tiled=True),
    )
    select = (slots_in.reshape(1, -1) == jnp.arange(owned_slots, dtype=jnp.int32)[:, None]).astype(
        jnp.bfloat16
    )
    partial_value = jnp.dot(
        select, received.reshape(-1, tile_width * tile_width), preferred_element_type=jnp.float32
    )
    partial_bf = partial_value.astype(jnp.bfloat16)
    owned_sums = lax.psum_scatter(
        partial_bf.astype(jnp.float32).astype(jnp.bfloat16), "term", scatter_dimension=0, tiled=True
    )
    comp_rotated = owned_sums.reshape(1, PAIR_DEV, tile_width, tile_width)
    return (normal_rotated, comp_rotated)


def solution(mesh):
    return jax.shard_map(
        on_device,
        mesh=mesh,
        in_specs=(
            P(("term", "pair"), None),
            P(("term", "pair"), None, None),
            P(("term", "pair"), None),
            P(("term", "pair"), None, None),
            P(("term", "pair"), None),
            P(("term", "pair"), None),
            P(("term", "pair")),
        ),
        out_specs=(P(("term", "pair"), None, None), P("pair", "term", None, None)),
        check_vma=False,
    )
```

profile of v0, /device:TPU:0, one launch (start us, length us, event | category | flops | bytes accessed | tf_op | source)
XLA Modules:
  0.0 625.8 jit_solution(5890029725378413766)
XLA Ops:
  7.2 0.0 all-gather.2.cloned.1.call-start
  7.2 0.7 all-gather.2.cloned.1.call-update
  7.9 0.7 fusion.17
  8.7 0.8 select_reduce_fusion.1
  9.5 0.7 multiply_add_fusion
  10.2 0.1 select_reduce_fusion
  10.3 0.7 sub.11
  10.9 4.6 all-to-all-start
  15.5 0.8 fusion.22
  16.3 195.9 %all-gather.2.cloned.1.call-done = bf16[12288,256]{1,0:T(8,128)(2,1)} async-done(((bf16[96,256]{1,0:T(8,128)(2,1)}), bf16[12288,256]{1,0:T(8,128)(2,1)}) %all-gather.2.cloned.1.call-update) | async-done | bytes 6291472 | tf_op jit(solution)/shard_map/all_gather | solution.py:21
  212.2 5.6 gather_fusion.2
  217.8 5.7 gather_fusion.3
  223.5 7.8 %fusion.13 = bf16[16,256,256]{2,1,0:T(8,128)(2,1)S(1)} fusion(bf16[16,512,256]{2,1,0:T(8,128)(2,1)} %gather_fusion.2, bf16[16,512,256]{2,1,0:T(8,128)(2,1)} %gather_fusion.3, bf16[16,512,512]{2,1,0:T(8,128)(2,1)} %param.10), kind=kOutput, calls=%fused_computation.15 | convolution fusion | flops 3224371200 | bytes 18874368 | tf_op jit(solution)/shard_map/nba,nbc->nac/dot_general | solution.py:15
  231.3 1.2 copy.25
  232.5 3.4 fusion
  235.8 0.0 all-to-all-done
  235.9 4.8 all-to-all-start.1
  240.7 0.0 all-reduce.3.cloned.1.call-start
  240.8 0.5 broadcast.80
  241.3 0.7 reduce.5
  241.9 0.1 eq.47
  242.0 48.4 %all-to-all-done.1 = bf16[4,8,65536]{2,1,0:T(8,128)(2,1)} async-done(((bf16[4,8,65536]{2,1,0:T(8,128)(2,1)}), bf16[4,8,65536]{2,1,0:T(8,128)(2,1)}, u32[]{:S(2)}, u32[]{:S(2)}) %all-to-all-start.1) | async-done | bytes 4194336 | tf_op jit(solution)/shard_map/all_to_all | solution.py:46
  290.4 5.5 convolution_convert_fusion
  295.9 0.0 copy-start.1
  295.9 0.0 copy-start
  295.9 0.0 all-reduce.3.cloned.1.call-update
  295.9 0.6 copy-done.1
  296.5 0.6 dynamic-slice
  297.1 0.0 copy-done
  297.1 5.6 gather_fusion.1
  302.7 5.6 gather_fusion
  308.3 8.8 %fusion.10 = bf16[16,256,256]{2,1,0:T(8,128)(2,1)} fusion(bf16[16,512,256]{2,1,0:T(8,128)(2,1)} %gather_fusion, bf16[16,512,256]{2,1,0:T(8,128)(2,1)} %gather_fusion.1, bf16[16,512,512]{2,1,0:T(8,128)(2,1)} %param.8), kind=kOutput, calls=%fused_computation.14 | convolution fusion | flops 3224371200 | bytes 18874368 | tf_op jit(solution)/shard_map/nba,nbc->nac/dot_general | solution.py:15
  317.2 298.4 %all-reduce.3.cloned.1.call-done = bf16[32,65536]{1,0:T(8,128)(2,1)} async-done(((bf16[32,65536]{1,0:T(8,128)(2,1)}), bf16[32,65536]{1,0:T(8,128)(2,1)}) %all-reduce.3.cloned.1.call-update) | async-done | bytes 4194320
  615.6 2.7 dynamic-slice_reduce_fusion
  618.3 0.7 reshape.52
  (5 shorter events, 0.1 us)
Async XLA Ops:
  7.2 205.0 %all-gather.2.cloned.1.call-start = ((), (), s32[]{:S(2)}) async-start(), calls=%async_computation.2 | async-start | bytes 6340608 | tf_op jit(solution)/shard_map/all_gather | solution.py:21
  10.9 224.9 %all-to-all-start = ((s32[4,1,8]{2,1,0:T(1,128)}), s32[4,1,8]{2,1,0:T(1,128)S(1)}, u32[]{:S(2)}, u32[]{:S(2)}) async-start(s32[4,1,8]{2,1,0:T(1,128)} %bitcast.4), calls=%async_computation | async-start | bytes 4096 | tf_op jit(solution)/shard_map/all_to_all | solution.py:47
  235.9 54.6 %all-to-all-start.1 = ((bf16[4,8,65536]{2,1,0:T(8,128)(2,1)}), bf16[4,8,65536]{2,1,0:T(8,128)(2,1)}, u32[]{:S(2)}, u32[]{:S(2)}) async-start(bf16[4,8,65536]{2,1,0:T(8,128)(2,1)} %fusion), calls=%async_computation.1 | async-start | bytes 8388608 | tf_op jit(solution)/shard_map/all_to_all | solution.py:46
  240.7 374.9 %all-reduce.3.cloned.1.call-start = ((), (), s32[]{:S(2)}) async-start(), calls=%async_computation.3 | async-start | bytes 8388608
  295.9 0.7 copy-start.1
  295.9 1.2 copy-start
Sparse Core Ops, SparseCore 0:
  9.7 202.4 all-gather.1
  296.0 319.5 all-reduce.2
where the time goes:
time: 626 us
  waiting for transfers between devices  543 us (87%)
  local copies, waits for them, and re-layouts  29.5 us (5%)
  matrix products  25.5 us (4%)
  between operations  14.1 us (2%)
  starting transfers between devices  9.5 us (2%)
    unnamed x3, waiting for transfers between devices  299 us
    all_gather x1, waiting for transfers between devices, on_device(): gathered = lax.all_gather(core_rows, ('term', 'pair'), axis=0, tiled=True)  196 us
    all_to_all x1, waiting for transfers between devices, on_device(): lax.all_to_all(outgoing, 'pair', split_axis=0, concat_axis=0, tiled=True)  48.4 us
    dot_general x2, matrix products, rotate_tiles(): jnp.einsum('nba,nbc->nac', left_rot, half_rotated, preferred_element_type...  16.7 us
  transfers between devices with their start and end apart: 4, of which 3 were waited for; matrix products, arithmetic and copies ran while one was open for 8% of the time, Pallas kernels for 0%

commit v1 on v0

--- a/solution.py
+++ b/solution.py
@@ -2,6 +2,7 @@
 import jax.numpy as jnp
 from jax import lax
 from jax.sharding import PartitionSpec as P
+from jax.lax import all_to_all, axis_size
 
 PAIR_DEV = 1
 
@@ -18,7 +19,8 @@
 def on_device(core_rows, norm_ops, norm_sectors, comp_ops, comp_sectors, comp_group, comp_slot):
     tile_width = core_rows.shape[1]
     row_width = norm_ops.shape[1]
-    gathered = lax.all_gather(core_rows, ("term", "pair"), axis=0, tiled=True)
+    val2 = jnp.stack(axis_size(("term", "pair")) * [core_rows], 0)
+    gathered = jnp.concatenate(all_to_all(val2, ("term", "pair"), 0, 0), 0)
     core_tiles = gathered.reshape(-1, row_width, tile_width)
     normal_rotated = rotate_tiles(core_tiles, norm_ops, norm_sectors).astype(jnp.bfloat16)
     groups = lax.axis_size("pair")

time: 626 us -> 525 us (0.84)
  waiting for transfers between devices: 543 us -> 429 us
  starting transfers between devices: 9.5 us -> 21.3 us
    all_gather x1 -> x0, waiting for transfers between devices: 196 us -> none  [on_device(): gathered = lax.all_gather(core_rows, ('term', 'pair'), axis=0, tiled=True)]
    all_to_all x0 -> x1, waiting for transfers between devices: none -> 78.4 us  [on_device(): gathered = jnp.concatenate(all_to_all(val2, ('term', 'pair'), 0, 0), 0)]
    all_to_all x0 -> x1, starting transfers between devices: none -> 11.6 us  [on_device(): gathered = jnp.concatenate(all_to_all(val2, ('term', 'pair'), 0, 0), 0)]
    unnamed x3 -> x2, waiting for transfers between devices: 299 us -> 302 us
  transfers between devices with their start and end apart: 4 -> 4, of which waited for: 3 -> 3; matrix products, arithmetic and copies ran while one was open for 8% -> 9% of each run, Pallas kernels for 0% -> 0%
where the time goes in v1:
time: 525 us
  waiting for transfers between devices  429 us (82%)
  local copies, waits for them, and re-layouts  33.8 us (6%)
  matrix products  25.4 us (5%)
  starting transfers between devices  21.3 us (4%)
  between operations  14.1 us (3%)
    unnamed x2, waiting for transfers between devices  302 us
    all_to_all x1, waiting for transfers between devices, on_device(): gathered = jnp.concatenate(all_to_all(val2, ('term', 'pair'), 0, 0), 0)  78.4 us
    all_to_all x1, waiting for transfers between devices, on_device(): lax.all_to_all(outgoing, 'pair', split_axis=0, concat_axis=0, tiled=True)  48.4 us
    dot_general x2, matrix products, rotate_tiles(): jnp.einsum('nba,nbc->nac', left_rot, half_rotated, preferred_element_type...  16.6 us
    all_to_all x1, starting transfers between devices, on_device(): gathered = jnp.concatenate(all_to_all(val2, ('term', 'pair'), 0, 0), 0)  11.6 us
    gather x2, local copies, waits for them, and re-layouts, rotate_tiles(): right_rot = core_tiles[sector_ids[:, 1]]  11.3 us
    gather x2, local copies, waits for them, and re-layouts, rotate_tiles(): left_rot = core_tiles[sector_ids[:, 0]]  11.2 us
  transfers between devices with their start and end apart: 4, of which 3 were waited for; matrix products, arithmetic and copies ran while one was open for 9% of the time, Pallas kernels for 0%

profile of v1, /device:TPU:0, one launch (start us, length us, event | category | flops | bytes accessed | tf_op | source)
XLA Modules:
  0.0 524.8 jit_solution(990809562243459844)
XLA Ops:
  7.2 4.2 stack.2
  11.4 0.0 copy-start
  11.4 0.0 copy-start.3
  11.4 0.0 copy-start.1
  11.4 11.6 %all-to-all-start = ((bf16[128,96,256]{2,1,0:T(8,128)(2,1)}), bf16[128,96,256]{2,1,0:T(8,128)(2,1)}, u32[]{:S(2)}, u32[]{:S(2)}) async-start(bf16[128,96,256]{2,1,0:T(8,128)(2,1)} %stack.2), calls=%async_computation | async-start | bytes 12582912 | tf_op jit(solution)/shard_map/all_to_all | solution.py:23
  23.1 0.0 copy-done
  23.1 0.1 fusion.17
  23.2 0.2 select_reduce_fusion.1
  23.4 0.0 copy-done.3
  23.4 0.1 select_reduce_fusion
  23.5 0.7 sub.11
  24.1 0.0 copy-done.1
  24.2 78.4 %all-to-all-done = bf16[128,96,256]{2,1,0:T(8,128)(2,1)} async-done(((bf16[128,96,256]{2,1,0:T(8,128)(2,1)}), bf16[128,96,256]{2,1,0:T(8,128)(2,1)}, u32[]{:S(2)}, u32[]{:S(2)}) %all-to-all-start) | async-done | bytes 6291488 | tf_op jit(solution)/shard_map/all_to_all | solution.py:23
  102.6 4.7 all-to-all-start.1
  107.3 5.6 %gather_fusion.2 = bf16[16,512,256]{2,1,0:T(8,128)(2,1)} fusion(bf16[24,512,256]{2,1,0:T(8,128)(2,1)} %bitcast, s32[1024]{0:T(1024)S(1)} %get-tuple-element.9), kind=kCustom, calls=%fused_computation.2 | custom fusion | bytes 8388672 | tf_op jit(solution)/shard_map/gather | solution.py:11
  113.0 5.7 %gather_fusion.3 = bf16[16,512,256]{2,1,0:T(8,128)(2,1)} fusion(bf16[24,512,256]{2,1,0:T(8,128)(2,1)} %bitcast, s32[1024]{0:T(1024)S(1)} %get-tuple-element.8), kind=kCustom, calls=%fused_computation.3 | custom fusion | bytes 8388672 | tf_op jit(solution)/shard_map/gather | solution.py:12
  118.6 7.8 %fusion.13 = bf16[16,256,256]{2,1,0:T(8,128)(2,1)S(1)} fusion(bf16[16,512,256]{2,1,0:T(8,128)(2,1)} %gather_fusion.2, bf16[16,512,256]{2,1,0:T(8,128)(2,1)} %gather_fusion.3, bf16[16,512,512]{2,1,0:T(8,128)(2,1)} %param.10), kind=kOutput, calls=%fused_computation.15 | convolution fusion | flops 3224371200 | bytes 18874368 | tf_op jit(solution)/shard_map/nba,nbc->nac/dot_general | solution.py:16
  126.4 1.2 copy.25
  127.6 3.4 fusion
  131.0 0.0 all-to-all-done.1
  131.0 4.8 all-to-all-start.2
  135.8 0.0 all-reduce.3.cloned.1.call-start
  135.9 0.5 broadcast.82
  136.4 0.7 reduce.5
  137.1 0.1 eq.47
  137.2 48.4 %all-to-all-done.2 = bf16[4,8,65536]{2,1,0:T(8,128)(2,1)} async-done(((bf16[4,8,65536]{2,1,0:T(8,128)(2,1)}), bf16[4,8,65536]{2,1,0:T(8,128)(2,1)}, u32[]{:S(2)}, u32[]{:S(2)}) %all-to-all-start.2) | async-done | bytes 4194336 | tf_op jit(solution)/shard_map/all_to_all | solution.py:48
  185.6 5.4 %convolution_convert_fusion = bf16[32,65536]{1,0:T(8,128)(2,1)} fusion(bf16[4,8,65536]{2,1,0:T(8,128)(2,1)} %all-to-all-done.2, s32[32]{0:T(128)S(1)} %eq.47), kind=kOutput, calls=%fused_computation.4 | convolution fusion | flops 136315904 | bytes 8388736 | tf_op jit(solution)/shard_map/dot_general | solution.py:54
  191.0 0.0 copy-start.4
  191.0 0.0 copy-start.2
  191.0 0.0 all-reduce.3.cloned.1.call-update
  191.0 0.6 copy-done.4
  191.7 0.6 dynamic-slice
  192.2 0.0 copy-done.2
  192.3 5.6 %gather_fusion.1 = bf16[16,512,256]{2,1,0:T(8,128)(2,1)} fusion(bf16[24,512,256]{2,1,0:T(8,128)(2,1)} %bitcast, s32[1024]{0:T(1024)S(1)} %get-tuple-element.6), kind=kCustom, calls=%fused_computation.1 | custom fusion | bytes 8388672 | tf_op jit(solution)/shard_map/gather | solution.py:12
  197.9 5.6 %gather_fusion = bf16[16,512,256]{2,1,0:T(8,128)(2,1)} fusion(bf16[24,512,256]{2,1,0:T(8,128)(2,1)} %bitcast, s32[1024]{0:T(1024)S(1)} %get-tuple-element.7), kind=kCustom, calls=%fused_computation | custom fusion | bytes 8388672 | tf_op jit(solution)/shard_map/gather | solution.py:11
  203.4 8.8 %fusion.10 = bf16[16,256,256]{2,1,0:T(8,128)(2,1)} fusion(bf16[16,512,256]{2,1,0:T(8,128)(2,1)} %gather_fusion, bf16[16,512,256]{2,1,0:T(8,128)(2,1)} %gather_fusion.1, bf16[16,512,512]{2,1,0:T(8,128)(2,1)} %param.8), kind=kOutput, calls=%fused_computation.14 | convolution fusion | flops 3224371200 | bytes 18874368 | tf_op jit(solution)/shard_map/nba,nbc->nac/dot_general | solution.py:16
  212.2 302.4 %all-reduce.3.cloned.1.call-done = bf16[32,65536]{1,0:T(8,128)(2,1)} async-done(((bf16[32,65536]{1,0:T(8,128)(2,1)}), bf16[32,65536]{1,0:T(8,128)(2,1)}) %all-reduce.3.cloned.1.call-update) | async-done | bytes 4194320
  514.6 2.7 dynamic-slice_reduce_fusion
  517.3 0.7 reshape.50
  (7 shorter events, 0.1 us)
Async XLA Ops:
  11.4 11.7 %copy-start = (s32[16,1]{0,1:T(1,128)S(1)}, s32[16,1]{0,1:T(1,128)}, u32[]{:S(2)}) copy-start(s32[16,1]{0,1:T(1,128)} %param.12) | copy-start | bytes 196
  11.4 12.0 %copy-start.3 = (s32[16]{0:T(128)S(1)}, s32[16]{0:T(128)}, u32[]{:S(2)}) copy-start(s32[16]{0:T(128)} %param.13) | copy-start | bytes 196
  11.4 12.7 %copy-start.1 = (s32[16,2]{0,1:T(2,128)S(1)}, s32[16,2]{0,1:T(2,128)}, u32[]{:S(2)}) copy-start(s32[16,2]{0,1:T(2,128)} %param.11) | copy-start | bytes 388
  11.4 91.2 %all-to-all-start = ((bf16[128,96,256]{2,1,0:T(8,128)(2,1)}), bf16[128,96,256]{2,1,0:T(8,128)(2,1)}, u32[]{:S(2)}, u32[]{:S(2)}) async-start(bf16[128,96,256]{2,1,0:T(8,128)(2,1)} %stack.2), calls=%async_computation | async-start | bytes 12582912 | tf_op jit(solution)/shard_map/all_to_all | solution.py:23
  102.6 28.4 %all-to-all-start.1 = ((s32[4,1,8]{2,1,0:T(1,128)}), s32[4,1,8]{2,1,0:T(1,128)S(1)}, u32[]{:S(2)}, u32[]{:S(2)}) async-start(s32[4,1,8]{2,1,0:T(1,128)} %bitcast.4), calls=%async_computation.1 | async-start | bytes 4096 | tf_op jit(solution)/shard_map/all_to_all | solution.py:49
  131.0 54.6 %all-to-all-start.2 = ((bf16[4,8,65536]{2,1,0:T(8,128)(2,1)}), bf16[4,8,65536]{2,1,0:T(8,128)(2,1)}, u32[]{:S(2)}, u32[]{:S(2)}) async-start(bf16[4,8,65536]{2,1,0:T(8,128)(2,1)} %fusion), calls=%async_computation.2 | async-start | bytes 8388608 | tf_op jit(solution)/shard_map/all_to_all | solution.py:48
  135.8 378.8 %all-reduce.3.cloned.1.call-start = ((), (), s32[]{:S(2)}) async-start(), calls=%async_computation.3 | async-start | bytes 8388608
  191.0 0.7 copy-start.4
  191.0 1.2 copy-start.2
Sparse Core Ops, SparseCore 0:
  191.1 323.4 all-reduce.2
